TPU v7x, 256 devices: a whole 4x4x8 slice. The times are simulated.
256 devices in a mesh: frame: 8 (over z_lo, x), brick: 32 (over y, z_hi, core).
Axes of the slice: x: 4, y: 4, z: 8 (z_hi: 4, z_lo: 2; z = z_hi * 2 + z_lo), core: 2. Of those that a mesh axis runs over, the one named last changes fastest.
Arguments:
- intensity: float32 [32, 512, 128], P('frame', 'brick'), may hold values from 0.1 to 10
- correction: float32 [32, 512, 128], P('frame', 'brick'), may hold values from 0.3 to 3
- splitting: bfloat16 [32, 32, 8, 128, 512], P('frame', 'brick'), may hold values from 0 to 0.015625
- block_count: int32 [32, 32], P('frame', 'brick'), may hold values from 1 to 8, 128 in all within a row
- pix_index: int32 [32, 32, 8], P('frame', 'brick'), may hold values from 0 to 511, as said below
- vox_offset: int32 [32, 32, 8], P('frame', 'brick'), may hold values from 0 to 129
Outputs:
- merged: float32 [32, 128, 512], P('brick', 'frame')
- weight: float32 [32, 128, 512], P('brick', 'frame')
Inputs may be any that keep to these rules, and one draw needn't show every extreme that they name: `block_count`: each frame's counts over the bricks sum to 128, and some pair of the frame holds 8. `pix_index`: the 32 slots of one device (its frames, its brick, padded slots included) include at most 4 slots (counted with repeats, over all of the device's frames) whose pixel block lies in the range 16 * c to 16 * c + 15, for every c; on every device some c has exactly 4 such slots.
All inputs are finite; a program needn't handle non-finite values. No bound on the sum of `block_count` on one device may be relied on, other than what follows from the above.
Results may differ from a plain program's by a relative error of at most 0.00049.
Values may be sent and summed in bfloat16 or wider, within the bound.
A program may use at most 64 MiB of HBM per device.

v0:
```python
import jax
import jax.numpy as jnp
from jax import lax
from jax.sharding import PartitionSpec as P

BLK_DEV = 16


def extended(block, sides, width):
    for axis, dim in sides:
        count = lax.axis_size(axis)
        forward = [(i, i + 1) for i in range(count - 1)]
        backward = [(target, source) for source, target in forward]
        low = lax.ppermute(
            lax.slice_in_dim(block, block.shape[dim] - width, None, axis=dim), axis, forward
        )
        high = lax.ppermute(lax.slice_in_dim(block, 0, width, axis=dim), axis, backward)
        block = jnp.concatenate([low, block, high], axis=dim)
    return block


def on_device(intensity, correction, splitting, block_count, pix_index, vox_offset):
    frames_dev, blocks_per_device, pixel_width = intensity.shape
    max_slots = splitting.shape[2]
    voxels = splitting.shape[4]
    bricks = lax.axis_size("brick")
    groups = lax.axis_size("frame")
    block_rows = BLK_DEV * groups
    slot_count = frames_dev * max_slots
    local_rows = jnp.stack([intensity, correction], axis=2).astype(jnp.bfloat16)
    indices = pix_index.reshape(slot_count)
    frame_slot = jnp.arange(slot_count, dtype=jnp.int32) // max_slots
    gathered = lax.all_gather(local_rows, "brick", axis=1, tiled=True)
    flat_rows = gathered.reshape(frames_dev * blocks_per_device * bricks, 2, pixel_width)
    rows_per_slot = flat_rows[frame_slot * (blocks_per_device * bricks) + indices]
    divided_blocks = splitting.reshape(slot_count, pixel_width, voxels)
    contrib = jnp.einsum(
        "edb,eba->eda", rows_per_slot, divided_blocks, preferred_element_type=jnp.float32
    )
    flat_contrib = contrib.reshape(slot_count, 2 * voxels)
    live_slots = (jnp.arange(max_slots, dtype=jnp.int32)[None, :] < block_count).reshape(slot_count)
    offsets = vox_offset.reshape(slot_count)
    edge_ids = jnp.array([0, block_rows + 1], dtype=jnp.int32)[:, None]
    edge_place = ((offsets[None, :] == edge_ids) & live_slots[None, :]).astype(jnp.float32)
    overhang = jnp.dot(
        edge_place,
        flat_contrib,
        precision=lax.Precision.HIGHEST,
        preferred_element_type=jnp.float32,
    ).reshape(2, 2, voxels)
    neighbours = extended(overhang, (("brick", 0),), 1)
    lower_add = neighbours[0]
    upper_increment = neighbours[3]
    row_ids = jnp.arange(1, block_rows + 1, dtype=jnp.int32)[:, None]
    placement = ((offsets[None, :] == row_ids) & live_slots[None, :]).astype(jnp.float32)
    interior = jnp.dot(
        placement, flat_contrib, precision=lax.Precision.HIGHEST, preferred_element_type=jnp.float32
    )
    interior = interior.reshape(block_rows, 2, voxels)
    interior = interior.at[0].add(lower_add).at[block_rows - 1].add(upper_increment)
    reduced = lax.psum_scatter(interior, "frame", scatter_dimension=0, tiled=True)
    weight = reduced[:, 1]
    merged = reduced[:, 0] / jnp.maximum(weight, 1.0)
    return (merged[None], weight[None])


def solution(mesh):
    placed = (
        P("frame", "brick", None),
        P("frame", "brick", None),
        P("frame", "brick", None, None, None),
        P("frame", "brick"),
        P("frame", "brick", None),
        P("frame", "brick", None),
    )
    return jax.shard_map(
        on_device,
        mesh=mesh,
        in_specs=placed,
        out_specs=(P("brick", "frame", None), P("brick", "frame", None)),
        check_vma=False,
    )
```

profile of v0, /device:TPU:8, one launch (start us, length us, event | category | flops | bytes accessed | tf_op | source)
XLA Modules:
  0.0 130.7 jit_solution(8027460333084453383)
XLA Ops:
  7.2 0.0 all-gather.2.cloned.1.call-start
  7.2 0.8 convert_bitcast_fusion
  8.0 0.6 pad_maximum_fusion
  8.6 0.0 all-gather.2.cloned.1.call-update
  8.6 0.0 reduce-scatter.2.cloned.1.call-start
  8.7 0.5 broadcast.132
  9.2 1.3 %reduce.10 = s32[4,8]{1,0:T(4,128)S(1)} reduce(s32[4,1,8]{2,1,0:T(1,128)} %param.15, s32[]{:T(128)} %broadcast.132), dimensions={1}, to_apply=%param.15.reduce_sub_computation.3 | reduce | bytes 260 | tf_op args[4]
  10.5 0.1 reshape.176
  10.6 1.3 %reduce.11 = s32[4,8]{1,0:T(4,128)S(1)} reduce(s32[4,1,8]{2,1,0:T(1,128)} %param.16, s32[]{:T(128)} %broadcast.132), dimensions={1}, to_apply=%param.16.reduce_sub_computation.3 | reduce | bytes 260 | tf_op args[5]
  12.0 0.1 eq.28
  12.1 0.7 iota_compare_fusion
  12.8 0.1 lt.37
  12.9 51.9 %all-gather.2.cloned.1.call-done = bf16[4,512,2,128]{3,1,0,2:T(8,128)(2,1)} async-done(((bf16[4,16,2,128]{3,1,0,2:T(8,128)(2,1)}), bf16[4,512,2,128]{3,1,0,2:T(8,128)(2,1)}) %all-gather.2.cloned.1.call-update) | async-done | bytes 1048592 | tf_op jit(solution)/shard_map/all_gather | solution.py:33
  64.8 2.3 %copy.9 = bf16[4,512,2,128]{3,2,1,0:T(2,128)(2,1)S(1)} copy(bf16[4,512,2,128]{3,1,0,2:T(8,128)(2,1)} %all-gather.2.cloned.1.call-done) | data formatting | bytes 2097152 | tf_op jit(solution)/shard_map/all_gather | solution.py:33
  67.1 0.6 gather_fusion
  67.7 2.8 %fusion.20 = f32[32,2,512]{2,1,0:T(2,128)S(1)} fusion(bf16[32,2,128]{2,1,0:T(2,128)(2,1)S(1)} %gather_fusion, bf16[32,128,512]{2,1,0:T(8,128)(2,1)} %bitcast.35), kind=kOutput, calls=%fused_computation.38 | convolution fusion | flops 8388608 | bytes 4341760 | tf_op jit(solution)/shard_map/edb,eba->eda/dot_general | solution.py:37
  70.6 0.2 fusion.10
  70.8 2.1 %collective-permute-start = (f32[1,2,512]{2,0,1:T(1,128)S(1)}, f32[1,2,512]{2,0,1:T(1,128)S(1)}, u32[]{:S(2)}, u32[]{:S(2)}) collective-permute-start(f32[1,2,512]{2,0,1:T(1,128)S(1)} %bitcast.41), channel_id=1, source_target_pairs={{0,1},{1,2},{2,3},{3,4},{4,5},{5,6},{6,7},{7,8},{8,9},{9,10},{10,1... | collective-permute-start | bytes 12296 | tf_op jit(solution)/shard_map/ppermute | solution.py:14
  73.0 0.5 fusion
  73.5 6.4 %collective-permute-start.1 = (f32[1,2,512]{2,0,1:T(1,128)S(1)}, f32[1,2,512]{2,0,1:T(1,128)S(1)}, u32[]{:S(2)}, u32[]{:S(2)}) collective-permute-start(f32[1,2,512]{2,0,1:T(1,128)S(1)} %bitcast.40), channel_id=1, source_target_pairs={{1,0},{2,1},{3,2},{4,3},{5,4},{6,5},{7,6},{8,7},{9,8},{10,9},{11,1... | collective-permute-start | bytes 12296 | tf_op jit(solution)/shard_map/ppermute | solution.py:17
  79.9 0.0 collective-permute-done
  79.9 0.1 scatter-add.6
  80.0 1.2 collective-permute-done.1
  81.2 0.1 scatter-add.9
  81.3 0.0 copy-start
  81.3 0.8 copy-done
  82.1 0.0 reduce-scatter.2.cloned.1.call-update
  82.1 40.4 %reduce-scatter.2.cloned.1.call-done = f32[16,2,512]{2,0,1:T(8,128)} async-done(((f32[128,2,512]{2,0,1:T(8,128)}), f32[16,2,512]{2,0,1:T(8,128)}) %reduce-scatter.2.cloned.1.call-update) | async-done | bytes 65552 | tf_op jit(solution)/shard_map/reduce_scatter | solution.py:61
  122.5 1.4 %fusion.3 = (f32[1,16,512]{2,1,0:T(8,128)}, f32[1,16,512]{2,1,0:T(8,128)}) fusion(f32[16,2,512]{2,0,1:T(8,128)} %reduce-scatter.2.cloned.1.call-done), kind=kLoop, calls=%fused_computation.6 | loop fusion | flops 16384 | bytes 131072 | tf_op jit(solution)/shard_map/div | solution.py:63
  (8 shorter events, 0.1 us)
Async XLA Ops:
  7.2 57.7 %all-gather.2.cloned.1.call-start = ((), (), s32[]{:S(2)}) async-start(), calls=%async_computation.1 | async-start | bytes 1081344 | tf_op jit(solution)/shard_map/all_gather | solution.py:33
  8.6 113.8 %reduce-scatter.2.cloned.1.call-start = ((), (), s32[]{:S(2)}) async-start(), calls=%async_computation.2 | async-start | bytes 589824 | tf_op jit(solution)/shard_map/reduce_scatter | solution.py:61
  70.8 9.1 %collective-permute-start = (f32[1,2,512]{2,0,1:T(1,128)S(1)}, f32[1,2,512]{2,0,1:T(1,128)S(1)}, u32[]{:S(2)}, u32[]{:S(2)}) collective-permute-start(f32[1,2,512]{2,0,1:T(1,128)S(1)} %bitcast.41), channel_id=1, source_target_pairs={{0,1},{1,2},{2,3},{3,4},{4,5},{5,6},{6,7},{7,8},{8,9},{9,10},{10,1... | collective-permute-start | bytes 12296 | tf_op jit(solution)/shard_map/ppermute | solution.py:14
  73.5 7.7 %collective-permute-start.1 = (f32[1,2,512]{2,0,1:T(1,128)S(1)}, f32[1,2,512]{2,0,1:T(1,128)S(1)}, u32[]{:S(2)}, u32[]{:S(2)}) collective-permute-start(f32[1,2,512]{2,0,1:T(1,128)S(1)} %bitcast.40), channel_id=1, source_target_pairs={{1,0},{2,1},{3,2},{4,3},{5,4},{6,5},{7,6},{8,7},{9,8},{10,9},{11,1... | collective-permute-start | bytes 12296 | tf_op jit(solution)/shard_map/ppermute | solution.py:17
  81.3 0.8 copy-start
Sparse Core Ops, SparseCore 0:
  11.0 53.7 all-gather.1
  82.2 40.1 reduce-scatter.1
where the time goes:
time: 131 us
  waiting for transfers between devices  93.5 us (71%)
  between operations  14.1 us (11%)
  starting transfers between devices  8.65 us (7%)
  other arithmetic  6.26 us (5%)
  local copies, waits for them, and re-layouts  4.63 us (4%)
  matrix products  3.52 us (3%)
    all_gather x1, waiting for transfers between devices, on_device(): gathered = lax.all_gather(local_rows, 'brick', axis=1, tiled=True)  51.9 us
    reduce_scatter x1, waiting for transfers between devices, on_device(): lax.psum_scatter(interior, 'frame', scatter_dimension=0, tiled=True)  40.4 us
    ppermute x1, starting transfers between devices, extended(): lax.ppermute(lax.slice_in_dim(block, 0, width, axis=dim), axis, backward)  6.43 us
    dot_general x1, matrix products, on_device(): jnp.einsum('edb,eba->eda', rows_per_slot, divided_blocks, preferred_eleme...  2.83 us
    unnamed x2, other arithmetic  2.69 us
  transfers between devices with their start and end apart: 4, of which 3 were waited for; matrix products, arithmetic and copies ran while one was open for 4% of the time, Pallas kernels for 0%

commit v1 on v0

--- a/solution.py
+++ b/solution.py
@@ -30,7 +30,9 @@
     local_rows = jnp.stack([intensity, correction], axis=2).astype(jnp.bfloat16)
     indices = pix_index.reshape(slot_count)
     frame_slot = jnp.arange(slot_count, dtype=jnp.int32) // max_slots
-    gathered = lax.all_gather(local_rows, "brick", axis=1, tiled=True)
+    gathered = jnp.concatenate(
+        lax.all_to_all(jnp.stack(lax.axis_size("brick") * [local_rows], axis=0), "brick", 0, 0), 1
+    )
     flat_rows = gathered.reshape(frames_dev * blocks_per_device * bricks, 2, pixel_width)
     rows_per_slot = flat_rows[frame_slot * (blocks_per_device * bricks) + indices]
     divided_blocks = splitting.reshape(slot_count, pixel_width, voxels)

time: 131 us -> 122 us (0.931)
  waiting for transfers between devices: 93.5 us -> 65.7 us
  starting transfers between devices: 8.65 us -> 20.3 us
  local copies, waits for them, and re-layouts: 4.63 us -> 12.4 us
    all_gather x1 -> x0, waiting for transfers between devices: 51.9 us -> none  [on_device(): gathered = lax.all_gather(local_rows, 'brick', axis=1, tiled=True)]
    all_to_all x0 -> x1, waiting for transfers between devices: none -> 23.4 us  [on_device(): lax.all_to_all(jnp.stack(lax.axis_size('brick') * [local_rows], axis=0),...]
    all_to_all x0 -> x1, starting transfers between devices: none -> 11.7 us  [on_device(): lax.all_to_all(jnp.stack(lax.axis_size('brick') * [local_rows], axis=0),...]
    another operation x0 -> x2, local copies, waits for them, and re-layouts: none -> 9.91 us  [the longest x1 8.68 us: on_device(): gathered.reshape(frames_dev * blocks_per_device * bricks, 2, pixel_width)]
    all_gather x1 -> x0, local copies, waits for them, and re-layouts: 2.3 us -> none  [on_device(): gathered = lax.all_gather(local_rows, 'brick', axis=1, tiled=True)]
where the time goes in v1:
time: 122 us
  waiting for transfers between devices  65.7 us (54%)
  starting transfers between devices  20.3 us (17%)
  between operations  14.1 us (12%)
  local copies, waits for them, and re-layouts  12.4 us (10%)
  other arithmetic  5.65 us (5%)
  matrix products  3.52 us (3%)
    reduce_scatter x1, waiting for transfers between devices, on_device(): lax.psum_scatter(interior, 'frame', scatter_dimension=0, tiled=True)  41.1 us
    all_to_all x1, waiting for transfers between devices, on_device(): lax.all_to_all(jnp.stack(lax.axis_size('brick') * [local_rows], axis=0),...  23.4 us
    all_to_all x1, starting transfers between devices, on_device(): lax.all_to_all(jnp.stack(lax.axis_size('brick') * [local_rows], axis=0),...  11.7 us
    another operation x1, local copies, waits for them, and re-layouts, on_device(): gathered.reshape(frames_dev * blocks_per_device * bricks, 2, pixel_width)  8.68 us
    ppermute x1, starting transfers between devices, extended(): lax.ppermute(lax.slice_in_dim(block, 0, width, axis=dim), axis, backward)  5.75 us
    dot_general x1, matrix products, on_device(): jnp.einsum('edb,eba->eda', rows_per_slot, divided_blocks, preferred_eleme...  2.83 us
    ppermute x1, starting transfers between devices, extended(): lax.ppermute(lax.slice_in_dim(block, block.shape[dim] - width, None, axis...  2.82 us
    unnamed x2, other arithmetic  2.69 us
  transfers between devices with their start and end apart: 4, of which 3 were waited for; matrix products, arithmetic and copies ran while one was open for 4% of the time, Pallas kernels for 0%

profile of v1, /device:TPU:8, one launch (start us, length us, event | category | flops | bytes accessed | tf_op | source)
XLA Modules:
  0.0 121.7 jit_solution(6521886235784570805)
XLA Ops:
  7.2 0.8 convert_bitcast_fusion
  8.0 1.2 %stack.11 = bf16[32,4,16,2,128]{4,2,1,3,0:T(8,128)(2,1)} broadcast(bf16[4,16,2,128]{3,1,0,2:T(8,128)(2,1)S(1)} %pad_maximum_fusion), dimensions={1,2,3,4} | broadcast | bytes 1081344 | tf_op jit(solution)/shard_map/stack | solution.py:34
  9.2 11.7 %all-to-all-start = ((bf16[32,4,16,2,128]{4,2,1,3,0:T(8,128)(2,1)}), bf16[32,4,16,2,128]{4,2,1,3,0:T(8,128)(2,1)S(1)}, u32[]{:S(2)}, u32[]{:S(2)}) async-start(bf16[32,4,16,2,128]{4,2,1,3,0:T(8,128)(2,1)} %stack.11), calls=%async_computation | async-start | bytes 2097152 | tf_op jit(solution)/shard_map/all_to_all | solution.py:34
  20.9 0.0 reduce-scatter.2.cloned.1.call-start
  20.9 0.5 broadcast.133
  21.5 1.3 %reduce.10 = s32[4,8]{1,0:T(4,128)S(1)} reduce(s32[4,1,8]{2,1,0:T(1,128)} %param.15, s32[]{:T(128)} %broadcast.133), dimensions={1}, to_apply=%param.15.reduce_sub_computation.3 | reduce | bytes 260 | tf_op args[4]
  22.8 0.1 reshape.187
  22.9 1.3 %reduce.11 = s32[4,8]{1,0:T(4,128)S(1)} reduce(s32[4,1,8]{2,1,0:T(1,128)} %param.16, s32[]{:T(128)} %broadcast.133), dimensions={1}, to_apply=%param.16.reduce_sub_computation.3 | reduce | bytes 260 | tf_op args[5]
  24.2 0.1 eq.28
  24.3 0.7 iota_compare_fusion
  25.1 0.1 lt.37
  25.2 23.4 %all-to-all-done = bf16[32,4,16,2,128]{4,2,1,3,0:T(8,128)(2,1)S(1)} async-done(((bf16[32,4,16,2,128]{4,2,1,3,0:T(8,128)(2,1)}), bf16[32,4,16,2,128]{4,2,1,3,0:T(8,128)(2,1)S(1)}, u32[]{:S(2)}, u32[]{:S(2)}) %all-to-all-start) | async-done | bytes 1048608 | tf_op jit(solution)/shard_map/all_to_all | solution.py:34
  48.6 0.2 copy.14
  48.8 8.7 %copy.15 = bf16[2048,2,128]{2,1,0:T(2,128)(2,1)S(1)} copy(bf16[2048,2,128]{2,0,1:T(8,128)(2,1)S(1)} %bitcast.38) | data formatting | bytes 2097152 | tf_op jit(solution)/shard_map/reshape;reshape | solution.py:36
  57.4 0.6 gather_fusion
  58.0 2.8 %fusion.20 = f32[32,2,512]{2,1,0:T(2,128)S(1)} fusion(bf16[32,2,128]{2,1,0:T(2,128)(2,1)S(1)} %gather_fusion, bf16[32,128,512]{2,1,0:T(8,128)(2,1)} %bitcast.37), kind=kOutput, calls=%fused_computation.38 | convolution fusion | flops 8388608 | bytes 4341760 | tf_op jit(solution)/shard_map/edb,eba->eda/dot_general | solution.py:39
  60.9 0.2 fusion.10
  61.1 2.8 %collective-permute-start = (f32[1,2,512]{2,0,1:T(1,128)S(1)}, f32[1,2,512]{2,0,1:T(1,128)S(1)}, u32[]{:S(2)}, u32[]{:S(2)}) collective-permute-start(f32[1,2,512]{2,0,1:T(1,128)S(1)} %bitcast.43), channel_id=1, source_target_pairs={{0,1},{1,2},{2,3},{3,4},{4,5},{5,6},{6,7},{7,8},{8,9},{9,10},{10,1... | collective-permute-start | bytes 12296 | tf_op jit(solution)/shard_map/ppermute | solution.py:14
  64.0 0.5 fusion
  64.5 5.8 %collective-permute-start.1 = (f32[1,2,512]{2,0,1:T(1,128)S(1)}, f32[1,2,512]{2,0,1:T(1,128)S(1)}, u32[]{:S(2)}, u32[]{:S(2)}) collective-permute-start(f32[1,2,512]{2,0,1:T(1,128)S(1)} %bitcast.42), channel_id=1, source_target_pairs={{1,0},{2,1},{3,2},{4,3},{5,4},{6,5},{7,6},{8,7},{9,8},{10,9},{11,1... | collective-permute-start | bytes 12296 | tf_op jit(solution)/shard_map/ppermute | solution.py:17
  70.2 0.0 collective-permute-done
  70.2 0.1 scatter-add.6
  70.3 1.2 collective-permute-done.1
  71.5 0.1 scatter-add.9
  71.6 0.0 copy-start
  71.6 0.8 copy-done
  72.4 0.0 reduce-scatter.2.cloned.1.call-update
  72.4 41.1 %reduce-scatter.2.cloned.1.call-done = f32[16,2,512]{2,0,1:T(8,128)} async-done(((f32[128,2,512]{2,0,1:T(8,128)}), f32[16,2,512]{2,0,1:T(8,128)}) %reduce-scatter.2.cloned.1.call-update) | async-done | bytes 65552 | tf_op jit(solution)/shard_map/reduce_scatter | solution.py:63
  113.5 1.4 %fusion.3 = (f32[1,16,512]{2,1,0:T(8,128)}, f32[1,16,512]{2,1,0:T(8,128)}) fusion(f32[16,2,512]{2,0,1:T(8,128)} %reduce-scatter.2.cloned.1.call-done), kind=kLoop, calls=%fused_computation.6 | loop fusion | flops 16384 | bytes 131072 | tf_op jit(solution)/shard_map/div | solution.py:65
  (9 shorter events, 0.1 us)
Async XLA Ops:
  9.2 39.4 %all-to-all-start = ((bf16[32,4,16,2,128]{4,2,1,3,0:T(8,128)(2,1)}), bf16[32,4,16,2,128]{4,2,1,3,0:T(8,128)(2,1)S(1)}, u32[]{:S(2)}, u32[]{:S(2)}) async-start(bf16[32,4,16,2,128]{4,2,1,3,0:T(8,128)(2,1)} %stack.11), calls=%async_computation | async-start | bytes 2097152 | tf_op jit(solution)/shard_map/all_to_all | solution.py:34
  20.9 92.6 %reduce-scatter.2.cloned.1.call-start = ((), (), s32[]{:S(2)}) async-start(), calls=%async_computation.2 | async-start | bytes 589824 | tf_op jit(solution)/shard_map/reduce_scatter | solution.py:63
  61.1 9.1 %collective-permute-start = (f32[1,2,512]{2,0,1:T(1,128)S(1)}, f32[1,2,512]{2,0,1:T(1,128)S(1)}, u32[]{:S(2)}, u32[]{:S(2)}) collective-permute-start(f32[1,2,512]{2,0,1:T(1,128)S(1)} %bitcast.43), channel_id=1, source_target_pairs={{0,1},{1,2},{2,3},{3,4},{4,5},{5,6},{6,7},{7,8},{8,9},{9,10},{10,1... | collective-permute-start | bytes 12296 | tf_op jit(solution)/shard_map/ppermute | solution.py:14
  64.5 7.1 %collective-permute-start.1 = (f32[1,2,512]{2,0,1:T(1,128)S(1)}, f32[1,2,512]{2,0,1:T(1,128)S(1)}, u32[]{:S(2)}, u32[]{:S(2)}) collective-permute-start(f32[1,2,512]{2,0,1:T(1,128)S(1)} %bitcast.42), channel_id=1, source_target_pairs={{1,0},{2,1},{3,2},{4,3},{5,4},{6,5},{7,6},{8,7},{9,8},{10,9},{11,1... | collective-permute-start | bytes 12296 | tf_op jit(solution)/shard_map/ppermute | solution.py:17
  71.6 0.8 copy-start
Sparse Core Ops, SparseCore 0:
  72.5 40.8 reduce-scatter.1
